TPU v7x, 32 devices: a whole 2x2x4 slice. The times are simulated.
32 devices in a mesh: gx: 8 (over y, x, core), gy: 4 (over z).
Axes of the slice: x: 2, y: 2, z: 4, core: 2. Of those that a mesh axis runs over, the one named last changes fastest.
Arguments:
- resid: bfloat16 [128, 16384], P(('gx', 'gy')), may hold values from -6 to 6
- query: bfloat16 [128, 16384], P(('gx', 'gy')), may hold values from -6 to 6
- key_new: bfloat16 [128, 1024], P(('gx', 'gy')), may hold values from -6 to 6
- value_new: bfloat16 [128, 1024], P(('gx', 'gy')), may hold values from -6 to 6
- cache_keys: bfloat16 [128, 128, 1024], P(('gx', 'gy'))
- cache_values: bfloat16 [128, 128, 1024], P(('gx', 'gy')), may hold values from -6 to 6
- lengths: int32 [128], P(('gx', 'gy')), may hold values from 1 to 128, as said below
- norm_gain: bfloat16 [16384], replicated, may hold values from 0.5 to 1.5
- gate_weight: bfloat16 [16384, 26624], P('gx', 'gy'), may hold values from -0.046875 to 0.046875
- up_weight: bfloat16 [16384, 26624], P('gx', 'gy'), may hold values from -0.046875 to 0.046875
- down_weight: bfloat16 [26624, 16384], P('gy', 'gx'), may hold values from -0.0390625 to 0.0390625
Outputs:
- layer_out: bfloat16 [128, 16384], P(('gx', 'gy'))
Inputs may be any that keep to these rules, and one draw needn't show every extreme that they name: `lengths`: some row has all 128 positions live.
All inputs are finite; a program needn't handle non-finite values.
Results may differ from a plain program's by a relative error of at most 0.0057.
Values may be sent and summed in bfloat16 or wider, within the bound.
A program may use at most 192 MiB of HBM per device.

v0:
```python
import jax
import jax.numpy as jnp
from jax import lax
from jax.sharding import PartitionSpec as P

HQ = 128
KV = 8
HD = 128


def attend_row(query, key_new, value_new, cache_keys, cache_values, length):
    scale_factor = HD ** (-0.5)
    span = cache_keys.shape[0]
    heads = query.astype(jnp.float32).reshape(KV, HQ // KV, HD)
    keys = cache_keys.reshape(span, KV, HD)
    values = cache_values.reshape(span, KV, HD)
    knew = key_new.astype(jnp.float32).reshape(KV, HD)
    vnew = value_new.astype(jnp.float32).reshape(KV, HD)
    scores = (
        jnp.einsum(
            "kgd,pkd->kgp",
            query.reshape(KV, HQ // KV, HD),
            keys,
            preferred_element_type=jnp.float32,
        )
        * scale_factor
    )
    places = jnp.arange(span, dtype=jnp.int32)
    scores = jnp.where(places[None, None, :] < length, scores, jnp.float32(-1e30))
    own = jnp.einsum("kgd,kd->kg", heads, knew) * scale_factor
    top = jnp.maximum(jnp.max(scores, axis=-1), own)
    expo = jnp.exp(scores - top[..., None])
    own_expo = jnp.exp(own - top)
    total = jnp.sum(expo, axis=-1) + own_expo
    probs = (expo / total[..., None]).astype(jnp.bfloat16)
    own_prob = (own_expo / total).astype(jnp.bfloat16).astype(jnp.float32)
    mixed = (
        jnp.einsum("kgp,pkd->kgd", probs, values, preferred_element_type=jnp.float32)
        + own_prob[..., None] * vnew[:, None, :]
    )
    return mixed.reshape(HQ * HD)


def on_device(
    resid,
    query,
    key_new,
    value_new,
    cache_keys,
    cache_values,
    lengths,
    norm_gain,
    gate_weight,
    up_weight,
    down_weight,
):
    attended = jax.vmap(attend_row)(query, key_new, value_new, cache_keys, cache_values, lengths)
    mid = (resid.astype(jnp.float32) + attended).astype(jnp.bfloat16)
    midf = mid.astype(jnp.float32)
    inverse = lax.rsqrt(jnp.mean(midf * midf, axis=-1, keepdims=True) + 1e-05)
    normed = (midf * inverse * norm_gain.astype(jnp.float32)).astype(jnp.bfloat16)
    stacked = jnp.stack([mid, normed], axis=1)
    blocks = lax.all_to_all(stacked, "gx", split_axis=2, concat_axis=0, tiled=True)
    gathered = lax.all_gather(blocks, "gy", axis=0, tiled=True)
    mid_rows = gathered[:, 0, :]
    normed_rows = gathered[:, 1, :]
    gate_part = jnp.dot(normed_rows, gate_weight, preferred_element_type=jnp.float32)
    up_part = jnp.dot(normed_rows, up_weight, preferred_element_type=jnp.float32)
    gate, up = lax.psum((gate_part, up_part), "gx")
    act = (jax.nn.silu(gate) * up).astype(jnp.bfloat16)
    block_rows = act.shape[0] // lax.axis_size("gy")
    ffn = lax.psum_scatter(
        jnp.dot(act, down_weight, preferred_element_type=jnp.float32),
        "gy",
        scatter_dimension=0,
        tiled=True,
    )
    own_mid = lax.dynamic_slice_in_dim(mid_rows, lax.axis_index("gy") * block_rows, block_rows, 0)
    finished = (own_mid.astype(jnp.float32) + ffn).astype(jnp.bfloat16)
    return lax.all_to_all(finished, "gx", split_axis=0, concat_axis=1, tiled=True)


def solution(mesh):
    placed = (
        P(("gx", "gy"), None),
        P(("gx", "gy"), None),
        P(("gx", "gy"), None),
        P(("gx", "gy"), None),
        P(("gx", "gy"), None, None),
        P(("gx", "gy"), None, None),
        P(("gx", "gy")),
        P(),
        P("gx", "gy"),
        P("gx", "gy"),
        P("gy", "gx"),
    )
    return jax.shard_map(
        on_device, mesh=mesh, in_specs=placed, out_specs=P(("gx", "gy"), None), check_vma=False
    )
```

profile of v0, /device:TPU:0, one launch (start us, length us, event | category | flops | bytes accessed | tf_op | source)
XLA Modules:
  0.0 320.8 jit_solution(10934704975294698136)
XLA Ops:
  6.5 0.8 iota_compare_fusion
  7.4 0.7 reshape.67
  8.1 0.7 convert_bitcast_fusion
  8.8 0.8 convert_element_type.45
  9.5 0.9 copy.32
  10.7 0.7 fusion.22
  11.4 0.3 fusion.14
  11.7 1.7 convolution_add_fusion
  13.4 0.3 fusion.9
  14.1 13.1 %copy.25 = bf16[4,2,16384]{0,1,2:T(2,128)(2,1)} copy(bf16[4,2,16384]{2,0,1:T(4,128)(2,1)S(1)} %pad_maximum_fusion) | data formatting | bytes 524288 | tf_op jit(solution)/shard_map/stack | solution.py:62
  27.2 16.2 %reshape.68 = bf16[8,2,8192]{2,1,0:T(2,128)(2,1)S(1)} reshape(bf16[16384,2,4]{2,1,0:T(2,128)(2,1)} %bitcast.58) | data formatting | bytes 524288
  43.4 11.9 %all_to_all.37 = bf16[8,2,8192]{2,1,0:T(2,128)(2,1)S(1)} all-to-all(bf16[8,2,8192]{2,1,0:T(2,128)(2,1)S(1)} %reshape.68), channel_id=1, replica_groups=mesh['gx'=8,'gy'=4] {'gx'}, dimensions={0} | all-to-all | bytes 524288 | tf_op jit(solution)/shard_map/all_to_all | solution.py:63
  55.3 19.1 %reshape.69 = bf16[16384,2,4]{2,1,0:T(2,128)(2,1)} reshape(bf16[8,2,8192]{2,1,0:T(2,128)(2,1)S(1)} %all_to_all.37) | data formatting | bytes 524288
  74.3 19.2 %copy.26 = bf16[4,2,8,2048]{3,0,2,1:T(4,128)(2,1)S(1)} copy(bf16[4,2,8,2048]{0,1,3,2:T(2,128)(2,1)} %bitcast.59) | data formatting | bytes 524288 | tf_op jit(solution)/shard_map/all_to_all | solution.py:63
  93.5 0.8 all_to_all.30
  94.5 27.2 %all-gather.2.cloned.1.call-done = bf16[128,2,2048]{2,0,1:T(8,128)(2,1)} async-done(((bf16[32,2,2048]{2,0,1:T(8,128)(2,1)}), bf16[128,2,2048]{2,0,1:T(8,128)(2,1)}) %all-gather.2.cloned.1.call-update) | async-done | bytes 1048592 | tf_op jit(solution)/shard_map/all_gather | solution.py:64
  121.8 14.5 %fusion.7 = f32[128,6656]{1,0:T(8,128)} fusion(bf16[2048,6656]{1,0:T(8,128)(2,1)} %param.20, bf16[128,2,2048]{2,0,1:T(8,128)(2,1)} %all-gather.2.cloned.1.call-done), kind=kOutput, calls=%fused_computation.11 | convolution fusion | flops 3489660928 | bytes 31195136 | tf_op jit(solution)/shard_map/dot_general | solution.py:68
  136.3 14.3 %fusion.8 = f32[128,6656]{1,0:T(8,128)} fusion(bf16[2048,6656]{1,0:T(8,128)(2,1)} %param.19, bf16[128,2,2048]{2,0,1:T(8,128)(2,1)S(1)} %copy-done.2), kind=kOutput, calls=%fused_computation.12 | convolution fusion | flops 3489660928 | bytes 31195136 | tf_op jit(solution)/shard_map/dot_general | solution.py:67
  150.6 109.8 %all-reduce.3.cloned.1.call-done = (f32[128,6656]{1,0:T(8,128)}, f32[128,6656]{1,0:T(8,128)}) async-done(((f32[128,6656]{1,0:T(8,128)}, f32[128,6656]{1,0:T(8,128)}), (f32[128,6656]{1,0:T(8,128)}, f32[128,6656]{1,0:T(8,128)})) %all-reduce.3.cloned.1.call-update) | async-done | bytes 6815760 | tf_op jit(solution)/shard_map/psum | solution.py:69
  260.4 15.7 %fusion = f32[128,2048]{1,0:T(8,128)} fusion(bf16[6656,2048]{1,0:T(8,128)(2,1)} %param.21, f32[128,6656]{1,0:T(8,128)} %get-tuple-element.5, f32[128,6656]{1,0:T(8,128)} %get-tuple-element.6), kind=kOutput, calls=%fused_computation.1 | convolution fusion | flops 3494772736 | bytes 35127296 | tf_op jit(solution)/shard_map/dot_general | solution.py:73
  276.2 27.4 %reduce-scatter.2.cloned.1.call-done = f32[32,2048]{1,0:T(8,128)} async-done(((f32[128,2048]{1,0:T(8,128)}), f32[32,2048]{1,0:T(8,128)}) %reduce-scatter.2.cloned.1.call-update) | async-done | bytes 262160 | tf_op jit(solution)/shard_map/reduce_scatter | solution.py:72
  303.6 1.0 fusion.13
  304.6 9.0 %all_to_all.38 = bf16[8,4,2048]{2,1,0:T(4,128)(2,1)S(1)} all-to-all(bf16[8,4,2048]{2,1,0:T(4,128)(2,1)S(1)} %all_to_all.31), channel_id=1, replica_groups=mesh['gx'=8,'gy'=4] {'gx'}, dimensions={0} | all-to-all | bytes 262144 | tf_op jit(solution)/shard_map/all_to_all | solution.py:80
  313.6 0.7 copy.52
  (24 shorter events, 0.9 us)
Async XLA Ops:
  6.5 4.1 %copy-start = (bf16[4,128,1024]{2,1,0:T(8,128)(2,1)S(1)}, bf16[4,128,1024]{2,1,0:T(8,128)(2,1)}, u32[]{:S(2)}) copy-start(bf16[4,128,1024]{2,1,0:T(8,128)(2,1)} %param.15) | copy-start | bytes 3145732
  6.5 6.8 %copy-start.3 = (bf16[4,16384]{1,0:T(4,128)(2,1)S(1)}, bf16[4,16384]{1,0:T(4,128)(2,1)}, u32[]{:S(2)}) copy-start(bf16[4,16384]{1,0:T(4,128)(2,1)} %param.11) | copy-start | bytes 393220
  6.5 115.2 %all-gather.2.cloned.1.call-start = ((), (), s32[]{:S(2)}) async-start(), calls=%async_computation.3 | async-start | bytes 1310720 | tf_op jit(solution)/shard_map/all_gather | solution.py:64
  94.3 166.1 %all-reduce.3.cloned.1.call-start = ((), (), s32[]{:S(2)}) async-start(), calls=%async_computation.5 | async-start | bytes 13631488 | tf_op jit(solution)/shard_map/psum | solution.py:69
  121.8 14.5 %copy-start.2 = (bf16[128,2,2048]{2,0,1:T(8,128)(2,1)S(1)}, bf16[128,2,2048]{2,0,1:T(8,128)(2,1)}, u32[]{:S(2)}) copy-start(bf16[128,2,2048]{2,0,1:T(8,128)(2,1)} %all-gather.2.cloned.1.call-done) | copy-start | bytes 3145732
  150.6 153.0 %reduce-scatter.2.cloned.1.call-start = ((), (), s32[]{:S(2)}) async-start(), calls=%async_computation.4 | async-start | bytes 1310720 | tf_op jit(solution)/shard_map/reduce_scatter | solution.py:72
  260.4 43.2 %slice-start = ((bf16[128,2,2048]{2,0,1:T(8,128)(2,1)}), bf16[128,1,2048]{2,0,1:T(8,128)(2,1)S(1)}, s32[]{:S(2)}) async-start(bf16[128,2,2048]{2,0,1:T(8,128)(2,1)} %all-gather.2.cloned.1.call-done), calls=%async_computation.6 | async-start | bytes 1048576 | tf_op jit(solution)/shard_map/slice | solution.py:65
  260.4 53.9 %copy-start.1 = (bf16[4,128,1024]{2,1,0:T(8,128)(2,1)S(1)}, bf16[4,128,1024]{2,1,0:T(8,128)(2,1)}, u32[]{:S(2)}) copy-start(bf16[4,128,1024]{2,1,0:T(8,128)(2,1)} %param.15) | copy-start | bytes 3145732
Sparse Core Ops, SparseCore 0:
  94.4 27.2 all-gather.1
  150.7 109.6 all-reduce.2
  276.3 27.2 reduce-scatter.1
where the time goes:
time: 322 us; the launch traced here: 321 us
  waiting for transfers between devices  164 us (51%)
  local copies, waits for them, and re-layouts  70.7 us (22%)
  matrix products  47.1 us (15%)
  blocking collectives  20.9 us (6%)
  between operations  13.2 us (4%)
  other arithmetic  4.23 us (1%)
    psum x1, waiting for transfers between devices, on_device(): gate, up = lax.psum((gate_part, up_part), 'gx')  110 us
    unnamed x13, local copies, waits for them, and re-layouts  36.9 us
    reduce_scatter x1, waiting for transfers between devices, on_device(): lax.psum_scatter(jnp.dot(act, down_weight, preferred_element_type=jnp.flo...  27.4 us
    all_gather x1, waiting for transfers between devices, on_device(): gathered = lax.all_gather(blocks, 'gy', axis=0, tiled=True)  27.2 us
    all_to_all x2, local copies, waits for them, and re-layouts, on_device(): lax.all_to_all(stacked, 'gx', split_axis=2, concat_axis=0, tiled=True)  20 us
    dot_general x1, matrix products, on_device(): jnp.dot(act, down_weight, preferred_element_type=jnp.float32)  15.7 us
    dot_general x1, matrix products, on_device(): jnp.dot(normed_rows, up_weight, preferred_element_type=jnp.float32)  14.5 us
    dot_general x1, matrix products, on_device(): jnp.dot(normed_rows, gate_weight, preferred_element_type=jnp.float32)  14.3 us
  transfers between devices with their start and end apart: 3, of which 3 were waited for; matrix products, arithmetic and copies ran while one was open for 0% of the time, Pallas kernels for 0%

commit v1 on v0

--- a/solution.py
+++ b/solution.py
@@ -60,7 +60,20 @@
     inverse = lax.rsqrt(jnp.mean(midf * midf, axis=-1, keepdims=True) + 1e-05)
     normed = (midf * inverse * norm_gain.astype(jnp.float32)).astype(jnp.bfloat16)
     stacked = jnp.stack([mid, normed], axis=1)
-    blocks = lax.all_to_all(stacked, "gx", split_axis=2, concat_axis=0, tiled=True)
+    seen_now = lax.axis_size("gx")
+    all_rows = lax.axis_index("gx")
+    w2, u_next = (seen_now, all_rows)
+    part_next = stacked.shape[2] // w2
+    before = list(stacked.shape)
+    before[2] = part_next
+    inter = before[0]
+    before[0] = inter * w2
+    blocks = jnp.zeros(before, stacked.dtype)
+    for j in [*range(w2)]:
+        high = lax.dynamic_slice_in_dim(stacked, (u_next ^ j) * part_next, part_next, axis=2)
+        if j:
+            high = lax.ppermute(high, "gx", [(w, w ^ j) for w in range(w2)])
+        blocks = lax.dynamic_update_slice_in_dim(blocks, high, (u_next ^ j) * inter, axis=0)
     gathered = lax.all_gather(blocks, "gy", axis=0, tiled=True)
     mid_rows = gathered[:, 0, :]
     normed_rows = gathered[:, 1, :]

time: 322 us -> 258 us (0.80)
  local copies, waits for them, and re-layouts: 70.7 us -> 3.28 us
  blocking collectives: 20.9 us -> 8.97 us
  waiting for transfers between devices: 164 us -> 172 us
  starting transfers between devices: 0.27 us -> 8.13 us
    unnamed x13, local copies, waits for them, and re-layouts: 36.9 us -> 2.29 us
    all_to_all x2 -> x0, local copies, waits for them, and re-layouts: 20 us -> none  [on_device(): lax.all_to_all(stacked, 'gx', split_axis=2, concat_axis=0, tiled=True)]
    another operation x1 -> x0, local copies, waits for them, and re-layouts: 13.1 us -> none  [on_device(): stacked = jnp.stack([mid, normed], axis=1)]
    all_to_all x1 -> x0, blocking collectives: 11.9 us -> none  [on_device(): lax.all_to_all(stacked, 'gx', split_axis=2, concat_axis=0, tiled=True)]
    ppermute x0 -> x7, starting transfers between devices: none -> 7.86 us  [on_device(): high = lax.ppermute(high, 'gx', [(w, w ^ j) for w in range(w2)])]
    ppermute x0 -> x7, waiting for transfers between devices: none -> 5.58 us  [on_device(): high = lax.ppermute(high, 'gx', [(w, w ^ j) for w in range(w2)])]
  transfers between devices with their start and end apart: 3 -> 10, of which waited for: 3 -> 5; matrix products, arithmetic and copies ran while one was open for 0% -> 0% of each run, Pallas kernels for 0% -> 0%
where the time goes in v1:
time: 258 us; the launch traced here: 257 us
  waiting for transfers between devices  172 us (67%)
  matrix products  47.2 us (18%)
  between operations  13.3 us (5%)
  blocking collectives  8.97 us (3%)
  starting transfers between devices  8.13 us (3%)
  other arithmetic  4.2 us (2%)
  local copies, waits for them, and re-layouts  3.28 us (1%)
    psum x1, waiting for transfers between devices, on_device(): gate, up = lax.psum((gate_part, up_part), 'gx')  110 us
    all_gather x1, waiting for transfers between devices, on_device(): gathered = lax.all_gather(blocks, 'gy', axis=0, tiled=True)  29.4 us
    reduce_scatter x1, waiting for transfers between devices, on_device(): lax.psum_scatter(jnp.dot(act, down_weight, preferred_element_type=jnp.flo...  27.4 us
    dot_general x1, matrix products, on_device(): jnp.dot(act, down_weight, preferred_element_type=jnp.float32)  15.8 us
    dot_general x1, matrix products, on_device(): jnp.dot(normed_rows, up_weight, preferred_element_type=jnp.float32)  14.6 us
    dot_general x1, matrix products, on_device(): jnp.dot(normed_rows, gate_weight, preferred_element_type=jnp.float32)  14.3 us
    all_to_all x1, blocking collectives, on_device(): lax.all_to_all(finished, 'gx', split_axis=0, concat_axis=1, tiled=True)  8.97 us
    ppermute x7, starting transfers between devices, on_device(): high = lax.ppermute(high, 'gx', [(w, w ^ j) for w in range(w2)])  7.86 us
  transfers between devices with their start and end apart: 10, of which 5 were waited for; matrix products, arithmetic and copies ran while one was open for 0% of the time, Pallas kernels for 0%

profile of v1, /device:TPU:0, one launch (start us, length us, event | category | flops | bytes accessed | tf_op | source)
XLA Modules:
  0.0 257.1 jit_solution(97644136628100007)
XLA Ops:
  6.5 0.8 iota_compare_fusion
  7.4 0.7 reshape.67
  8.1 0.7 convert_bitcast_fusion
  8.8 0.8 convert_element_type.45
  9.5 0.9 copy.19
  10.7 0.7 fusion.31
  11.7 1.7 convolution_add_fusion
  14.0 0.5 collective-permute-start
  14.6 3.6 %collective-permute-start.5 = (bf16[4,2,2048]{2,0,1:T(4,128)(2,1)S(1)}, bf16[4,2,2048]{2,0,1:T(4,128)(2,1)S(1)}, u32[]{:S(2)}, u32[]{:S(2)}) collective-permute-start(bf16[4,2,2048]{2,0,1:T(4,128)(2,1)S(1)} %get-tuple-element.14), channel_id=1, source_target_pairs={{0,24},{4,28},{8,16},{12,20},{16,8},{20,12},{24,0},{28,4},{1,25},{... | collective-permute-start | bytes 98312 | tf_op jit(solution)/shard_map/ppermute | solution.py:75
  18.2 0.5 collective-permute-start.3
  18.7 1.0 collective-permute-start.4
  20.0 1.9 collective-permute-start.1
  21.9 2.2 collective-permute-done.1
  24.2 3.4 %collective-permute-done.2 = bf16[4,2,2048]{2,0,1:T(4,128)(2,1)S(1)} collective-permute-done((bf16[4,2,2048]{2,0,1:T(4,128)(2,1)S(1)}, bf16[4,2,2048]{2,0,1:T(4,128)(2,1)S(1)}, u32[]{:S(2)}, u32[]{:S(2)}) %collective-permute-start.2) | collective-permute-done | bytes 32800 | tf_op jit(solution)/shard_map/ppermute | solution.py:75
  27.8 0.7 copy-done.3
  28.6 29.4 %all-gather.2.cloned.1.call-done = bf16[128,2,2048]{2,0,1:T(8,128)(2,1)} async-done(((bf16[32,2,2048]{2,0,1:T(8,128)(2,1)}), bf16[128,2,2048]{2,0,1:T(8,128)(2,1)}) %all-gather.2.cloned.1.call-update) | async-done | bytes 1048592 | tf_op jit(solution)/shard_map/all_gather | solution.py:77
  57.9 14.6 %fusion.7 = f32[128,6656]{1,0:T(8,128)} fusion(bf16[2048,6656]{1,0:T(8,128)(2,1)} %param.20, bf16[128,2,2048]{2,0,1:T(8,128)(2,1)} %all-gather.2.cloned.1.call-done), kind=kOutput, calls=%fused_computation.11 | convolution fusion | flops 3489660928 | bytes 31195136 | tf_op jit(solution)/shard_map/dot_general | solution.py:81
  72.5 14.3 %fusion.8 = f32[128,6656]{1,0:T(8,128)} fusion(bf16[2048,6656]{1,0:T(8,128)(2,1)} %param.19, bf16[128,2,2048]{2,0,1:T(8,128)(2,1)S(1)} %copy-done.2), kind=kOutput, calls=%fused_computation.12 | convolution fusion | flops 3489660928 | bytes 31195136 | tf_op jit(solution)/shard_map/dot_general | solution.py:80
  87.1 109.6 %all-reduce.3.cloned.1.call-done = (f32[128,6656]{1,0:T(8,128)}, f32[128,6656]{1,0:T(8,128)}) async-done(((f32[128,6656]{1,0:T(8,128)}, f32[128,6656]{1,0:T(8,128)}), (f32[128,6656]{1,0:T(8,128)}, f32[128,6656]{1,0:T(8,128)})) %all-reduce.3.cloned.1.call-update) | async-done | bytes 6815760 | tf_op jit(solution)/shard_map/psum | solution.py:82
  196.7 15.8 %fusion = f32[128,2048]{1,0:T(8,128)} fusion(bf16[6656,2048]{1,0:T(8,128)(2,1)} %param.21, f32[128,6656]{1,0:T(8,128)} %get-tuple-element.5, f32[128,6656]{1,0:T(8,128)} %get-tuple-element.6), kind=kOutput, calls=%fused_computation.1 | convolution fusion | flops 3494772736 | bytes 35127296 | tf_op jit(solution)/shard_map/dot_general | solution.py:86
  212.5 27.4 %reduce-scatter.2.cloned.1.call-done = f32[32,2048]{1,0:T(8,128)} async-done(((f32[128,2048]{1,0:T(8,128)}), f32[32,2048]{1,0:T(8,128)}) %reduce-scatter.2.cloned.1.call-update) | async-done | bytes 262160 | tf_op jit(solution)/shard_map/reduce_scatter | solution.py:85
  239.9 1.0 fusion.13
  240.9 9.0 %all_to_all.19 = bf16[8,4,2048]{2,1,0:T(4,128)(2,1)S(1)} all-to-all(bf16[8,4,2048]{2,1,0:T(4,128)(2,1)S(1)} %all_to_all.14), channel_id=1, replica_groups=mesh['gx'=8,'gy'=4] {'gx'}, dimensions={0} | all-to-all | bytes 262144 | tf_op jit(solution)/shard_map/all_to_all | solution.py:93
  249.9 0.7 copy.47
  (43 shorter events, 2.1 us)
Async XLA Ops:
  6.5 4.1 %copy-start = (bf16[4,128,1024]{2,1,0:T(8,128)(2,1)S(1)}, bf16[4,128,1024]{2,1,0:T(8,128)(2,1)}, u32[]{:S(2)}) copy-start(bf16[4,128,1024]{2,1,0:T(8,128)(2,1)} %param.15) | copy-start | bytes 3145732
  6.5 6.8 %copy-start.4 = (bf16[4,16384]{1,0:T(4,128)(2,1)S(1)}, bf16[4,16384]{1,0:T(4,128)(2,1)}, u32[]{:S(2)}) copy-start(bf16[4,16384]{1,0:T(4,128)(2,1)} %param.11) | copy-start | bytes 393220
  6.5 51.4 %all-gather.2.cloned.1.call-start = ((), (), s32[]{:S(2)}) async-start(), calls=%async_computation.2 | async-start | bytes 1310720 | tf_op jit(solution)/shard_map/all_gather | solution.py:77
  14.0 6.0 %collective-permute-start = (bf16[4,2,2048]{2,0,1:T(4,128)(2,1)S(1)}, bf16[4,2,2048]{2,0,1:T(4,128)(2,1)S(1)}, u32[]{:S(2)}, u32[]{:S(2)}) collective-permute-start(bf16[4,2,2048]{2,0,1:T(4,128)(2,1)S(1)} %get-tuple-element.11), channel_id=1, source_target_pairs={{0,4},{4,0},{8,12},{12,8},{16,20},{20,16},{24,28},{28,24},{1,5},{5... | collective-permute-start | bytes 98312 | tf_op jit(solution)/shard_map/ppermute | solution.py:75
  14.6 13.1 %collective-permute-start.5 = (bf16[4,2,2048]{2,0,1:T(4,128)(2,1)S(1)}, bf16[4,2,2048]{2,0,1:T(4,128)(2,1)S(1)}, u32[]{:S(2)}, u32[]{:S(2)}) collective-permute-start(bf16[4,2,2048]{2,0,1:T(4,128)(2,1)S(1)} %get-tuple-element.14), channel_id=1, source_target_pairs={{0,24},{4,28},{8,16},{12,20},{16,8},{20,12},{24,0},{28,4},{1,25},{... | collective-permute-start | bytes 98312 | tf_op jit(solution)/shard_map/ppermute | solution.py:75
  18.2 9.4 %collective-permute-start.3 = (bf16[4,2,2048]{2,0,1:T(4,128)(2,1)S(1)}, bf16[4,2,2048]{2,0,1:T(4,128)(2,1)S(1)}, u32[]{:S(2)}, u32[]{:S(2)}) collective-permute-start(bf16[4,2,2048]{2,0,1:T(4,128)(2,1)S(1)} %get-tuple-element.15), channel_id=1, source_target_pairs={{0,16},{4,20},{8,24},{12,28},{16,0},{20,4},{24,8},{28,12},{1,17},{... | collective-permute-start | bytes 98312 | tf_op jit(solution)/shard_map/ppermute | solution.py:75
  18.7 9.0 %collective-permute-start.4 = (bf16[4,2,2048]{2,0,1:T(4,128)(2,1)S(1)}, bf16[4,2,2048]{2,0,1:T(4,128)(2,1)S(1)}, u32[]{:S(2)}, u32[]{:S(2)}) collective-permute-start(bf16[4,2,2048]{2,0,1:T(4,128)(2,1)S(1)} %get-tuple-element.16), channel_id=1, source_target_pairs={{0,20},{4,16},{8,28},{12,24},{16,4},{20,0},{24,12},{28,8},{1,21},{... | collective-permute-start | bytes 98312 | tf_op jit(solution)/shard_map/ppermute | solution.py:75
  19.7 8.1 %collective-permute-start.6 = (bf16[4,2,2048]{2,0,1:T(4,128)(2,1)S(1)}, bf16[4,2,2048]{2,0,1:T(4,128)(2,1)S(1)}, u32[]{:S(2)}, u32[]{:S(2)}) collective-permute-start(bf16[4,2,2048]{2,0,1:T(4,128)(2,1)S(1)} %get-tuple-element.9), channel_id=1, source_target_pairs={{0,28},{4,24},{8,20},{12,16},{16,12},{20,8},{24,4},{28,0},{1,29},{... | collective-permute-start | bytes 98312 | tf_op jit(solution)/shard_map/ppermute | solution.py:75
  20.0 4.1 %collective-permute-start.1 = (bf16[4,2,2048]{2,0,1:T(4,128)(2,1)S(1)}, bf16[4,2,2048]{2,0,1:T(4,128)(2,1)S(1)}, u32[]{:S(2)}, u32[]{:S(2)}) collective-permute-start(bf16[4,2,2048]{2,0,1:T(4,128)(2,1)S(1)} %get-tuple-element.12), channel_id=1, source_target_pairs={{0,8},{4,12},{8,0},{12,4},{16,24},{20,28},{24,16},{28,20},{1,9},{5... | collective-permute-start | bytes 98312 | tf_op jit(solution)/shard_map/ppermute | solution.py:75
  24.1 3.5 %collective-permute-start.2 = (bf16[4,2,2048]{2,0,1:T(4,128)(2,1)S(1)}, bf16[4,2,2048]{2,0,1:T(4,128)(2,1)S(1)}, u32[]{:S(2)}, u32[]{:S(2)}) collective-permute-start(bf16[4,2,2048]{2,0,1:T(4,128)(2,1)S(1)} %get-tuple-element.13), channel_id=1, source_target_pairs={{0,12},{4,8},{8,4},{12,0},{16,28},{20,24},{24,20},{28,16},{1,13},{... | collective-permute-start | bytes 98312 | tf_op jit(solution)/shard_map/ppermute | solution.py:75
  27.8 0.7 copy-start.3
  28.5 168.2 %all-reduce.3.cloned.1.call-start = ((), (), s32[]{:S(2)}) async-start(), calls=%async_computation.4 | async-start | bytes 13631488 | tf_op jit(solution)/shard_map/psum | solution.py:82
  57.9 14.6 %copy-start.2 = (bf16[128,2,2048]{2,0,1:T(8,128)(2,1)S(1)}, bf16[128,2,2048]{2,0,1:T(8,128)(2,1)}, u32[]{:S(2)}) copy-start(bf16[128,2,2048]{2,0,1:T(8,128)(2,1)} %all-gather.2.cloned.1.call-done) | copy-start | bytes 3145732
  86.9 153.0 %reduce-scatter.2.cloned.1.call-start = ((), (), s32[]{:S(2)}) async-start(), calls=%async_computation.3 | async-start | bytes 1310720 | tf_op jit(solution)/shard_map/reduce_scatter | solution.py:85
  196.7 43.2 %slice-start = ((bf16[128,2,2048]{2,0,1:T(8,128)(2,1)}), bf16[128,1,2048]{2,0,1:T(8,128)(2,1)S(1)}, s32[]{:S(2)}) async-start(bf16[128,2,2048]{2,0,1:T(8,128)(2,1)} %all-gather.2.cloned.1.call-done), calls=%async_computation.5 | async-start | bytes 1048576 | tf_op jit(solution)/shard_map/slice | solution.py:78
  196.7 53.9 %copy-start.1 = (bf16[4,128,1024]{2,1,0:T(8,128)(2,1)S(1)}, bf16[4,128,1024]{2,1,0:T(8,128)(2,1)}, u32[]{:S(2)}) copy-start(bf16[4,128,1024]{2,1,0:T(8,128)(2,1)} %param.15) | copy-start | bytes 3145732
Sparse Core Ops, SparseCore 0:
  28.6 29.2 all-gather.1
  87.0 109.6 all-reduce.2
  212.6 27.2 reduce-scatter.1
